TPU v7x, 32 devices: a whole 2x2x4 slice. The times are simulated.
32 devices in a mesh: dp: 8 (over y, x, core), tp: 4 (over z).
Axes of the slice: x: 2, y: 2, z: 4, core: 2. Of those that a mesh axis runs over, the one named last changes fastest.
Arguments:
- tokens: bfloat16 [16384, 2048], P('dp'), may hold values from -6 to 6
- doc_ids: int32 [16, 1024], P('dp'), may hold values from 0 to 3, never falling along the last dimension, each value on 1 to 512 neighbouring positions
- norm1_gain: bfloat16 [2048], replicated, may hold values from 0.5 to 1.5
- norm1_bias: bfloat16 [2048], replicated, may hold values from -4 to 4
- query_weight: bfloat16 [2048, 2048], P(None, 'tp'), may hold values from -0.125 to 0.125
- query_bias: bfloat16 [2048], P('tp'), may hold values from -6 to 6
- keyval_weight: bfloat16 [2048, 256], replicated, may hold values from -0.125 to 0.125
- value_bias: bfloat16 [128], replicated, may hold values from -3 to 3
- out_weight: bfloat16 [2048, 2048], P('tp'), may hold values from -0.5 to 0.5
- out_bias: bfloat16 [2048], replicated, may hold values from -6 to 6
- norm2_gain: bfloat16 [2048], replicated, may hold values from 0.5 to 1.5
- norm2_bias: bfloat16 [2048], replicated, may hold values from -4 to 4
- up_weight: bfloat16 [2048, 8192], P(None, 'tp'), may hold values from -0.125 to 0.125
- up_bias: bfloat16 [8192], P('tp'), may hold values from -6 to 6
- down_weight: bfloat16 [8192, 2048], P('tp'), may hold values from -0.0625 to 0.0625
- down_bias: bfloat16 [2048], replicated, may hold values from -6 to 6
- grad_out: bfloat16 [16384, 2048], P('dp'), may hold values from -6 to 6
Outputs:
- output: bfloat16 [16384, 2048], P('dp')
- grad_tokens: bfloat16 [16384, 2048], P('dp')
- grad_norm1_gain: float32 [2048], P('dp')
- grad_norm1_bias: float32 [2048], P('dp')
- grad_query_weight: float32 [2048, 2048], P('dp', 'tp')
- grad_query_bias: float32 [2048], P(('tp', 'dp'))
- grad_keyval_weight: float32 [2048, 256], P(('dp', 'tp'))
- grad_value_bias: float32 [128], P(('dp', 'tp'))
- grad_out_weight: float32 [2048, 2048], P('tp', 'dp')
- grad_out_bias: float32 [2048], P('dp')
- grad_norm2_gain: float32 [2048], P('dp')
- grad_norm2_bias: float32 [2048], P('dp')
- grad_up_weight: float32 [2048, 8192], P('dp', 'tp')
- grad_up_bias: float32 [8192], P(('tp', 'dp'))
- grad_down_weight: float32 [8192, 2048], P('tp', 'dp')
- grad_down_bias: float32 [2048], P('dp')
Inputs may be any that keep to these rules, and one draw needn't show every extreme that they name: `doc_ids`: document numbers never fall along a row of a window; a document spans 1 to half of 1024 tokens.
All inputs are finite; a program needn't handle non-finite values.
Results may differ from a plain program's by a relative error of at most 0.02.
Values may be sent and summed in bfloat16 or wider, within the bound.
A program may use at most 384 MiB of HBM per device.

v0:
```python
import jax
import jax.numpy as jnp
from jax import lax
from jax.sharding import PartitionSpec as P


def layer_norm(values, gain_vec, shift_vec):
    center = values - jnp.mean(values, axis=-1, keepdims=True)
    spread = jnp.mean(center * center, axis=-1, keepdims=True)
    return center * lax.rsqrt(spread + 1e-05) * gain_vec + shift_vec


def gelu_tanh(values):
    return jax.nn.gelu(values, approximate=True)


def allowed_mask(doc_row):
    places = jnp.arange(doc_row.shape[0])
    return (doc_row[:, None] == doc_row[None, :]) & (places[:, None] >= places[None, :])


def masked_scores(heads_q, keys_low, allowed, score_scale):
    scores = (
        jnp.einsum("shd,td->hst", heads_q, keys_low, preferred_element_type=jnp.float32)
        * score_scale
    )
    return jnp.where(allowed[None], scores, -1e30)


def forward_block(seq_rows, doc_row, params, score_scale, head_dim):
    seq_len = seq_rows.shape[0]
    normed1 = layer_norm(seq_rows, params["norm1_gain"], params["norm1_bias"]).astype(jnp.bfloat16)
    queries = (
        jnp.dot(normed1, params["query_weight"], preferred_element_type=jnp.float32)
        + params["query_bias"]
    )
    heads_q = queries.astype(jnp.bfloat16).reshape(seq_len, -1, head_dim)
    keyval = jnp.dot(normed1, params["keyval_weight"], preferred_element_type=jnp.float32)
    keys_low = keyval[:, :head_dim].astype(jnp.bfloat16)
    values_low = (keyval[:, head_dim:] + params["value_bias"]).astype(jnp.bfloat16)
    allowed = allowed_mask(doc_row)
    scores = masked_scores(heads_q, keys_low, allowed, score_scale)
    highest = jnp.max(scores, axis=2, keepdims=True)
    lifted = jnp.exp(scores - highest)
    totals = jnp.sum(lifted, axis=2, keepdims=True)
    chances = lifted / totals
    log_totals = (highest + jnp.log(totals))[..., 0]
    attended = (
        jnp.einsum(
            "hst,td->shd",
            chances.astype(jnp.bfloat16),
            values_low,
            preferred_element_type=jnp.float32,
        )
        .astype(jnp.bfloat16)
        .reshape(seq_len, -1)
    )
    partial_value = jnp.dot(attended, params["out_weight"], preferred_element_type=jnp.float32)
    mixed_sum = lax.psum(partial_value.astype(jnp.bfloat16), "tp").astype(jnp.float32)
    hidden1 = seq_rows + mixed_sum + params["out_bias"]
    normed2 = layer_norm(hidden1, params["norm2_gain"], params["norm2_bias"]).astype(jnp.bfloat16)
    before = (
        jnp.dot(normed2, params["up_weight"], preferred_element_type=jnp.float32)
        + params["up_bias"]
    )
    activated = gelu_tanh(before).astype(jnp.bfloat16)
    down_part = jnp.dot(activated, params["down_weight"], preferred_element_type=jnp.float32)
    summed = lax.psum(down_part.astype(jnp.bfloat16), "tp").astype(jnp.float32)
    result = hidden1 + summed + params["down_bias"]
    kept_state = (
        normed1,
        heads_q,
        keys_low,
        values_low,
        allowed,
        log_totals,
        attended,
        hidden1,
        normed2,
        before,
        activated,
    )
    return (result, kept_state)


def backward_block(seq_rows, cotangent, kept_state, params, score_scale, head_dim):
    (
        normed1,
        heads_q,
        keys_low,
        values_low,
        allowed,
        log_totals,
        attended,
        hidden1,
        normed2,
        before,
        activated,
    ) = kept_state
    seq_len = seq_rows.shape[0]
    grad_low = cotangent.astype(jnp.bfloat16)
    grad_down_bias = jnp.sum(cotangent, axis=0)
    grad_down_weight = jnp.dot(activated.T, grad_low, preferred_element_type=jnp.float32)
    grad_activated = jnp.dot(grad_low, params["down_weight"].T, preferred_element_type=jnp.float32)
    grad_before = jax.vjp(gelu_tanh, before)[1](grad_activated)[0].astype(jnp.bfloat16)
    grad_up_weight = jnp.dot(normed2.T, grad_before, preferred_element_type=jnp.float32)
    grad_up_bias = jnp.sum(grad_before.astype(jnp.float32), axis=0)
    partial2 = jnp.dot(grad_before, params["up_weight"].T, preferred_element_type=jnp.float32)
    grad_normed2 = lax.psum(partial2.astype(jnp.bfloat16), "tp").astype(jnp.float32)
    norm2_pull = jax.vjp(layer_norm, hidden1, params["norm2_gain"], params["norm2_bias"])[1]
    through2, grad_norm2_gain, grad_norm2_bias = norm2_pull(grad_normed2)
    grad_hidden1 = cotangent + through2
    grad_out_bias = jnp.sum(grad_hidden1, axis=0)
    grad_mixed = grad_hidden1.astype(jnp.bfloat16)
    grad_out_weight = jnp.dot(attended.T, grad_mixed, preferred_element_type=jnp.float32)
    grad_attended = jnp.dot(grad_mixed, params["out_weight"].T, preferred_element_type=jnp.float32)
    grad_attended = grad_attended.astype(jnp.bfloat16).reshape(seq_len, -1, head_dim)
    scores = masked_scores(heads_q, keys_low, allowed, score_scale)
    chances = jnp.exp(scores - log_totals[..., None])
    grad_chances = jnp.einsum(
        "shd,td->hst", grad_attended, values_low, preferred_element_type=jnp.float32
    )
    grad_values = jnp.einsum(
        "hst,shd->td",
        chances.astype(jnp.bfloat16),
        grad_attended,
        preferred_element_type=jnp.float32,
    )
    weighted = jnp.sum(chances * grad_chances, axis=2, keepdims=True)
    grad_scores = (chances * (grad_chances - weighted) * score_scale).astype(jnp.bfloat16)
    grad_queries = jnp.einsum(
        "hst,td->shd", grad_scores, keys_low, preferred_element_type=jnp.float32
    )
    grad_queries = grad_queries.reshape(seq_len, -1).astype(jnp.bfloat16)
    grad_keys = jnp.einsum("hst,shd->td", grad_scores, heads_q, preferred_element_type=jnp.float32)
    grad_keyval = jnp.concatenate([grad_keys, grad_values], axis=1).astype(jnp.bfloat16)
    grad_query_weight = jnp.dot(normed1.T, grad_queries, preferred_element_type=jnp.float32)
    grad_query_bias = jnp.sum(grad_queries.astype(jnp.float32), axis=0)
    grad_keyval_weight = jnp.dot(normed1.T, grad_keyval, preferred_element_type=jnp.float32)
    grad_value_bias = jnp.sum(grad_keyval[:, head_dim:].astype(jnp.float32), axis=0)
    partial1 = jnp.dot(grad_queries, params["query_weight"].T, preferred_element_type=jnp.float32)
    partial1 = partial1 + jnp.dot(
        grad_keyval, params["keyval_weight"].T, preferred_element_type=jnp.float32
    )
    grad_normed1 = lax.psum(partial1.astype(jnp.bfloat16), "tp").astype(jnp.float32)
    norm1_pull = jax.vjp(layer_norm, seq_rows, params["norm1_gain"], params["norm1_bias"])[1]
    through1, grad_norm1_gain, grad_norm1_bias = norm1_pull(grad_normed1)
    grad_input = grad_hidden1 + through1
    grad_terms = (
        grad_query_weight,
        grad_up_weight,
        grad_query_bias,
        grad_up_bias,
        grad_norm1_gain,
        grad_norm1_bias,
        grad_out_bias,
        grad_norm2_gain,
        grad_norm2_bias,
        grad_down_bias,
        grad_out_weight,
        grad_down_weight,
        grad_keyval_weight,
        grad_value_bias,
    )
    return (grad_input, grad_terms)


def reduce_once(grad_terms):
    row_shards = (
        lax.psum_scatter(
            grad_terms[0].astype(jnp.bfloat16), "dp", scatter_dimension=0, tiled=True
        ).astype(jnp.float32),
        lax.psum_scatter(
            grad_terms[1].astype(jnp.bfloat16), "dp", scatter_dimension=0, tiled=True
        ).astype(jnp.float32),
        lax.psum_scatter(
            grad_terms[2].astype(jnp.bfloat16), "dp", scatter_dimension=0, tiled=True
        ).astype(jnp.float32),
        lax.psum_scatter(
            grad_terms[3].astype(jnp.bfloat16), "dp", scatter_dimension=0, tiled=True
        ).astype(jnp.float32),
        lax.psum_scatter(
            grad_terms[4].astype(jnp.bfloat16), "dp", scatter_dimension=0, tiled=True
        ).astype(jnp.float32),
        lax.psum_scatter(
            grad_terms[5].astype(jnp.bfloat16), "dp", scatter_dimension=0, tiled=True
        ).astype(jnp.float32),
        lax.psum_scatter(
            grad_terms[6].astype(jnp.bfloat16), "dp", scatter_dimension=0, tiled=True
        ).astype(jnp.float32),
        lax.psum_scatter(
            grad_terms[7].astype(jnp.bfloat16), "dp", scatter_dimension=0, tiled=True
        ).astype(jnp.float32),
        lax.psum_scatter(
            grad_terms[8].astype(jnp.bfloat16), "dp", scatter_dimension=0, tiled=True
        ).astype(jnp.float32),
        lax.psum_scatter(
            grad_terms[9].astype(jnp.bfloat16), "dp", scatter_dimension=0, tiled=True
        ).astype(jnp.float32),
    )
    col_shards = (
        lax.psum_scatter(
            grad_terms[10].astype(jnp.bfloat16), "dp", scatter_dimension=1, tiled=True
        ).astype(jnp.float32),
        lax.psum_scatter(
            grad_terms[11].astype(jnp.bfloat16), "dp", scatter_dimension=1, tiled=True
        ).astype(jnp.float32),
    )
    shared_shards = (
        lax.psum_scatter(grad_terms[12], ("dp", "tp"), scatter_dimension=0, tiled=True),
        lax.psum_scatter(grad_terms[13], ("dp", "tp"), scatter_dimension=0, tiled=True),
    )
    return tuple(row_shards) + tuple(col_shards) + tuple(shared_shards)


def per_device(
    tokens,
    doc_ids,
    norm1_gain,
    norm1_bias,
    query_weight,
    query_bias,
    keyval_weight,
    value_bias,
    out_weight,
    out_bias,
    norm2_gain,
    norm2_bias,
    up_weight,
    up_bias,
    down_weight,
    down_bias,
    grad_out,
):
    micro_count = doc_ids.shape[0]
    seq_len = doc_ids.shape[1]
    head_dim = value_bias.shape[0]
    score_scale = head_dim ** (-0.5)
    params = {
        "norm1_gain": norm1_gain.astype(jnp.float32),
        "norm1_bias": norm1_bias.astype(jnp.float32),
        "query_weight": query_weight,
        "query_bias": query_bias.astype(jnp.float32),
        "keyval_weight": keyval_weight,
        "value_bias": value_bias.astype(jnp.float32),
        "out_weight": out_weight,
        "out_bias": out_bias.astype(jnp.float32),
        "norm2_gain": norm2_gain.astype(jnp.float32),
        "norm2_bias": norm2_bias.astype(jnp.float32),
        "up_weight": up_weight,
        "up_bias": up_bias.astype(jnp.float32),
        "down_weight": down_weight,
        "down_bias": down_bias.astype(jnp.float32),
    }
    results = []
    input_grads = []
    running = None
    for micro_index in range(micro_count):
        seq_rows = tokens[micro_index * seq_len : (micro_index + 1) * seq_len].astype(jnp.float32)
        cotangent = grad_out[micro_index * seq_len : (micro_index + 1) * seq_len].astype(
            jnp.float32
        )
        result, kept_state = forward_block(
            seq_rows, doc_ids[micro_index], params, score_scale, head_dim
        )
        results.append(result.astype(jnp.bfloat16))
        grad_input, grad_terms = backward_block(
            seq_rows, cotangent, kept_state, params, score_scale, head_dim
        )
        input_grads.append(grad_input.astype(jnp.bfloat16))
        if running is None:
            running = grad_terms
        else:
            running = tuple((current + incoming for current, incoming in zip(running, grad_terms)))
    running = reduce_once(running)
    return (
        jnp.concatenate(results, axis=0),
        jnp.concatenate(input_grads, axis=0),
        running[4],
        running[5],
        running[0],
        running[2],
        running[12],
        running[13],
        running[10],
        running[6],
        running[7],
        running[8],
        running[1],
        running[3],
        running[11],
        running[9],
    )


def solution(mesh):
    return jax.shard_map(
        per_device,
        mesh=mesh,
        in_specs=(
            P("dp", None),
            P("dp", None),
            P(),
            P(),
            P(None, "tp"),
            P("tp"),
            P(),
            P(),
            P("tp", None),
            P(),
            P(),
            P(),
            P(None, "tp"),
            P("tp"),
            P("tp", None),
            P(),
            P("dp", None),
        ),
        out_specs=(
            P("dp", None),
            P("dp", None),
            P("dp"),
            P("dp"),
            P("dp", "tp"),
            P(("tp", "dp")),
            P(("dp", "tp"), None),
            P(("dp", "tp")),
            P("tp", "dp"),
            P("dp"),
            P("dp"),
            P("dp"),
            P("dp", "tp"),
            P(("tp", "dp")),
            P("tp", "dp"),
            P("dp"),
        ),
        check_vma=False,
    )
```

profile of v0, /device:TPU:0, one launch (start us, length us, event | category | flops | bytes accessed | tf_op | source)
XLA Modules:
  0.0 1856.1 jit_solution(11825210403797541873)
XLA Ops:
  53.8 157.1 %all-reduce.17.cloned.1.call-done = bf16[1024,2048]{1,0:T(8,128)(2,1)} async-done(((bf16[1024,2048]{1,0:T(8,128)(2,1)}), bf16[1024,2048]{1,0:T(8,128)(2,1)}) %all-reduce.17.cloned.1.call-update) | async-done | bytes 4194320 | tf_op jit(solution)/shard_map/psum | solution.py:59
  254.4 154.0 %all-reduce.19.cloned.1.call-done = bf16[1024,2048]{1,0:T(8,128)(2,1)} async-done(((bf16[1024,2048]{1,0:T(8,128)(2,1)}), bf16[1024,2048]{1,0:T(8,128)(2,1)}) %all-reduce.19.cloned.1.call-update) | async-done | bytes 4194320 | tf_op jit(solution)/shard_map/psum | solution.py:59
  421.3 15.1 fusion.162
  436.4 21.1 %convert_reduce_fusion.8 = (f32[2048]{0:T(1024)}, bf16[1024,2048]{1,0:T(8,128)(2,1)}) fusion(f32[1024,2048]{1,0:T(8,128)} %fusion.162, f32[2048]{0:T(1024)S(1)} %convert_element_type.317, bf16[2048,2048]{1,0:T(8,128)(2,1)} %param.31, bf16[2048,2048]{1,0:T(8,128)(2,1)} %param.33), kind=kOutput, calls=%fused_computation.106 | convolution fusion | flops 8638167040 | bytes 25182208 | tf_op jit(solution)/shard_map/dot_general | solution.py:104
  457.5 14.1 convolution_convert_fusion
  485.5 19.2 %convert_reduce_fusion.9 = (f32[2048]{0:T(1024)}, bf16[1024,2048]{1,0:T(8,128)(2,1)S(1)}) fusion(f32[1024,2048]{1,0:T(8,128)} %fusion.161, f32[2048]{0:T(1024)S(1)} %convert_element_type.317, bf16[2048,2048]{1,0:T(8,128)(2,1)} %param.31, bf16[2048,2048]{1,0:T(8,128)(2,1)} %param.33), kind=kOutput, calls=%fused_computation.107 | convolution fusion | flops 8638167040 | bytes 25182208 | tf_op jit(solution)/shard_map/dot_general | solution.py:104
  520.2 289.9 %all-reduce.23.cloned.1.call-done = (bf16[1024,2048]{1,0:T(8,128)(2,1)}, bf16[1024,2048]{1,0:T(8,128)(2,1)}) async-done(((bf16[1024,2048]{1,0:T(8,128)(2,1)}, bf16[1024,2048]{1,0:T(8,128)(2,1)}), (bf16[1024,2048]{1,0:T(8,128)(2,1)}, bf16[1024,2048]{1,0:T(8,128)(2,1)})) %all-reduce.23.cloned.1.call-update) | async-done | bytes 8388624 | tf_op jit(solution)/shard_map/psum | solution.py:109
  835.7 14.1 fusion.168
  873.3 26.1 %convert_reduce_fusion.10 = (f32[128,4]{0,1:T(4,128)}, bf16[128,4,1024]{2,0,1:T(8,128)(2,1)}) fusion(f32[1024,1024,4]{1,0,2:T(8,128)} %fusion.135, f32[4,1024,1024]{1,2,0:T(8,128)} %get-tuple-element.75, f32[4,1024]{1,0:T(4,128)S(1)} %log_add_fusion, f32[1024,256]{1,0:T(8,128)} %copy-done.32), kind=kOutput, calls=%fused_computation.155 | convolution fusion | flops 1104679424 | bytes 68454400 | tf_op jit(solution)/shard_map/hst,td->shd/dot_general | solution.py:131
  914.4 24.0 %convert_reduce_fusion.11 = (f32[128,4]{0,1:T(4,128)}, bf16[128,4,1024]{2,0,1:T(8,128)(2,1)S(1)}) fusion(f32[1024,1024,4]{1,0,2:T(8,128)} %fusion.138, f32[4,1024,1024]{1,2,0:T(8,128)} %get-tuple-element.73, f32[4,1024]{1,0:T(4,128)S(1)} %log_add_fusion.1, f32[1024,256]{1,0:T(8,128)S(1)} %copy-done.31), kind=kOutput, calls=%fused_computation.156 | convolution fusion | flops 1104679424 | bytes 68454400 | tf_op jit(solution)/shard_map/hst,td->shd/dot_general | solution.py:131
  947.2 20.6 %fusion.85 = f32[2048,2048]{1,0:T(8,128)} fusion(bf16[2048,2048]{1,0:T(8,128)(2,1)} %param.33, f32[1024,2048]{1,0:T(8,128)} %fusion.161, f32[2048]{0:T(1024)S(1)} %convert_element_type.317), kind=kOutput, calls=%fused_computation.150 | convolution fusion | flops 8610906112 | bytes 29368320 | tf_op jit(solution)/shard_map/dot_general | solution.py:103
  967.8 21.9 %add_convert_fusion = bf16[2048,2048]{1,0:T(8,128)(2,1)} fusion(f32[2048,2048]{1,0:T(8,128)} %fusion.85, bf16[2048,2048]{1,0:T(8,128)(2,1)} %param.33, f32[1024,2048]{1,0:T(8,128)} %fusion.162, f32[2048]{0:T(1024)S(1)} %convert_element_type.317), kind=kOutput, calls=%fused_computation.14 | convolution fusion | flops 8619294720 | bytes 37756928 | tf_op jit(solution)/shard_map/dot_general | solution.py:103
  990.4 17.5 fusion.160
  1007.9 17.5 add_convert_fusion.1
  1025.4 16.5 convolution_convert_fusion.2
  1041.9 16.0 convolution_convert_fusion.4
  1058.0 26.8 %fusion.123 = bf16[1024,128]{0,1:T(8,128)(2,1)S(1)} fusion(bf16[1024,4,128]{0,2,1:T(8,128)(2,1)S(1)} %bitcast.204, f32[1024,1024,4]{1,0,2:T(8,128)} %fusion.135, f32[4,1024,1024]{1,2,0:T(8,128)} %get-tuple-element.75, f32[4,1024]{1,0:T(4,128)S(1)} %copy-done.38), kind=kOutput, calls=%fused_computation.179 | convolution fusion | flops 1103238144 | bytes 34881536 | tf_op jit(solution)/shard_map/hst,shd->td/dot_general | solution.py:135
  1084.9 24.9 %fusion.122 = bf16[1024,128]{0,1:T(8,128)(2,1)S(1)} fusion(bf16[1024,4,128]{0,2,1:T(8,128)(2,1)S(1)} %bitcast.202, f32[1024,1024,4]{1,0,2:T(8,128)} %fusion.138, f32[4,1024,1024]{1,2,0:T(8,128)} %get-tuple-element.73, f32[4,1024]{1,0:T(4,128)S(1)} %copy-done.36), kind=kOutput, calls=%fused_computation.178 | convolution fusion | flops 1103238144 | bytes 34881536 | tf_op jit(solution)/shard_map/hst,shd->td/dot_general | solution.py:135
  1151.2 43.5 %all-reduce.3 = f32[128]{0:T(128)S(1)} all-reduce(f32[128]{0:T(128)S(1)} %add.343), channel_id=7, replica_groups=mesh['dp'=8,'tp'=4] {'dp','tp'}, use_global_device_ids=true, to_apply=%region_43.44.clone | all-reduce | flops 128 | bytes 1024
  1213.1 496.3 %all-reduce.21.cloned.1.call-done = (bf16[1024,2048]{1,0:T(8,128)(2,1)}, bf16[1024,2048]{1,0:T(8,128)(2,1)}, bf16[1024,2048]{1,0:T(8,128)(2,1)}, bf16[1024,2048]{1,0:T(8,128)(2,1)}) async-done(((bf16[1024,2048]{1,0:T(8,128)(2,1)}, bf16[1024,2048]{1,0:T(8,128)(2,1)}, bf16[1024,2048]{1,0:T(8,128)(2,1)}, bf16[1024,2048]{1,0:T(8,128)(2,1)}), (bf16[1024,2048]{1,0:T(8,128)(2,1)}, bf16[1024,2048]{1,0:T(8,128)(2,1)}, ...) | async-done | bytes 16777232 | tf_op jit(solution)/shard_map/psum | solution.py:68
  1720.2 15.9 fusion.55
  1736.2 25.3 %all-reduce.9 = (bf16[2048]{0:T(1024)(128)(2,1)S(1)}, bf16[2048]{0:T(1024)(128)(2,1)S(1)}, bf16[512]{0:T(512)(128)(2,1)S(1)}, bf16[2048]{0:T(1024)(128)(2,1)S(1)...) all-reduce(bf16[2048]{0:T(1024)(128)(2,1)S(1)} %add_convert_fusion., ...), channel_id=2, replica_groups=mesh['dp'=8,'tp'=4] {'dp'}, use_global_device_ids=true, to_apply=%region_32.33.clone | all-reduce | flops 14848 | bytes 59392
  1766.5 16.8 add_convert_fusion.4
  1800.5 48.8 %reduce-scatter.8.cloned.1.call-done = f32[64,256]{1,0:T(8,128)} async-done(((f32[2048,256]{1,0:T(8,128)}), f32[64,256]{1,0:T(8,128)}) %reduce-scatter.8.cloned.1.call-update) | async-done | bytes 65552 | tf_op jit(solution)/shard_map/reduce_scatter | solution.py:210
  (312 shorter events, 296.4 us)
Async XLA Ops:
  7.2 203.7 %all-reduce.17.cloned.1.call-start = ((), (), s32[]{:S(2)}) async-start(), calls=%async_computation.5 | async-start | bytes 8388608 | tf_op jit(solution)/shard_map/psum | solution.py:59
  8.1 232.8 %copy-start.71 = (f32[128]{0:T(128)}, f32[128]{0:T(128)S(1)}, u32[]{:S(2)}) copy-start(f32[128]{0:T(128)S(1)} %convert_element_type.304) | copy-start | bytes 1540
  13.0 204.1 %copy-start.33 = (f32[2048]{0:T(1024)}, f32[2048]{0:T(1024)S(1)}, u32[]{:S(2)}) copy-start(f32[2048]{0:T(1024)S(1)} %convert_element_type.301) | copy-start | bytes 24580
  53.1 355.4 %all-reduce.19.cloned.1.call-start = ((), (), s32[]{:S(2)}) async-start(), calls=%async_computation.6 | async-start | bytes 8388608 | tf_op jit(solution)/shard_map/psum | solution.py:59
  53.2 168.5 %copy-start.41 = (f32[1024]{0:T(1024)}, f32[1024]{0:T(1024)S(1)}, u32[]{:S(2)}) copy-start(f32[1024]{0:T(1024)S(1)} %broadcast_multiply_fusion.1) | copy-start | bytes 12292
  254.3 555.9 %all-reduce.23.cloned.1.call-start = ((), (), s32[]{:S(2)}) async-start(), calls=%async_computation.13 | async-start | bytes 16777216 | tf_op jit(solution)/shard_map/psum | solution.py:109
  254.4 217.2 %copy-start.61 = (f32[2048]{0:T(1024)}, f32[2048]{0:T(1024)S(1)}, u32[]{:S(2)}) copy-start(f32[2048]{0:T(1024)S(1)} %convert_element_type.315) | copy-start | bytes 24580
  519.5 684.5 %reduce-scatter.10.cloned.1.call-start = ((), (), s32[]{:S(2)}) async-start(), calls=%async_computation.9 | async-start | bytes 2359296 | tf_op jit(solution)/shard_map/reduce_scatter | solution.py:202
  520.2 394.2 %copy-start.35 = (f32[4,1024]{1,0:T(4,128)}, f32[4,1024]{1,0:T(4,128)S(1)}, u32[]{:S(2)}) copy-start(f32[4,1024]{1,0:T(4,128)S(1)} %log_add_fusion.1) | copy-start | bytes 49156
  520.2 353.1 %copy-start.37 = (f32[4,1024]{1,0:T(4,128)}, f32[4,1024]{1,0:T(4,128)S(1)}, u32[]{:S(2)}) copy-start(f32[4,1024]{1,0:T(4,128)S(1)} %log_add_fusion) | copy-start | bytes 49156
  863.4 342.3 %reduce-scatter.6.cloned.1.call-start = ((), (), s32[]{:S(2)}) async-start(), calls=%async_computation.7 | async-start | bytes 2359296 | tf_op jit(solution)/shard_map/reduce_scatter | solution.py:170
  947.1 260.4 %reduce-scatter.14.cloned.1.call-start = ((), (), s32[]{:S(2)}) async-start(), calls=%async_computation.11 | async-start | bytes 9437184 | tf_op jit(solution)/shard_map/reduce_scatter | solution.py:205
  989.7 220.5 %reduce-scatter.12.cloned.1.call-start = ((), (), s32[]{:S(2)}) async-start(), calls=%async_computation.10 | async-start | bytes 9437184 | tf_op jit(solution)/shard_map/reduce_scatter | solution.py:173
  1025.4 684.0 %all-reduce.21.cloned.1.call-start = ((), (), s32[]{:S(2)}) async-start(), calls=%async_computation.12 | async-start | bytes 33554432 | tf_op jit(solution)/shard_map/psum | solution.py:68
  1143.3 52.0 %copy-start.73 = (f32[128,4]{0,1:T(4,128)S(1)}, f32[128,4]{0,1:T(4,128)}, u32[]{:S(2)}) copy-start(f32[128,4]{0,1:T(4,128)} %get-tuple-element.78) | copy-start | bytes 6148
  1143.3 52.0 %copy-start.57 = (f32[2048]{0:T(1024)S(1)}, f32[2048]{0:T(1024)}, u32[]{:S(2)}) copy-start(f32[2048]{0:T(1024)} %get-tuple-element.18) | copy-start | bytes 24580
  1143.3 52.0 %copy-start.58 = (f32[2048]{0:T(1024)S(1)}, f32[2048]{0:T(1024)}, u32[]{:S(2)}) copy-start(f32[2048]{0:T(1024)} %get-tuple-element.25) | copy-start | bytes 24580
  1143.4 52.0 %copy-start.59 = (f32[2048]{0:T(1024)S(1)}, f32[2048]{0:T(1024)}, u32[]{:S(2)}) copy-start(f32[2048]{0:T(1024)} %get-tuple-element.60) | copy-start | bytes 24580
  1143.4 52.0 %copy-start.60 = (f32[2048]{0:T(1024)S(1)}, f32[2048]{0:T(1024)}, u32[]{:S(2)}) copy-start(f32[2048]{0:T(1024)} %get-tuple-element.62) | copy-start | bytes 24580
  1143.4 706.0 %reduce-scatter.8.cloned.1.call-start = ((), (), s32[]{:S(2)}) async-start(), calls=%async_computation.8 | async-start | bytes 2162688 | tf_op jit(solution)/shard_map/reduce_scatter | solution.py:210
  1199.0 510.4 %copy-start.34 = (f32[2048]{0:T(1024)S(1)}, f32[2048]{0:T(1024)}, u32[]{:S(2)}) copy-start(f32[2048]{0:T(1024)} %copy-done.33) | copy-start | bytes 24580
  1199.0 510.4 %copy-start.40 = (f32[1024]{0:T(1024)S(1)}, f32[1024]{0:T(1024)}, u32[]{:S(2)}) copy-start(f32[1024]{0:T(1024)} %copy-done.39) | copy-start | bytes 12292
  1199.0 510.4 %copy-start.42 = (f32[1024]{0:T(1024)S(1)}, f32[1024]{0:T(1024)}, u32[]{:S(2)}) copy-start(f32[1024]{0:T(1024)} %copy-done.41) | copy-start | bytes 12292
  1791.8 57.5 %copy-start.1 = (bf16[512,2048]{1,0:T(8,128)(2,1)S(1)}, bf16[512,2048]{1,0:T(8,128)(2,1)}, u32[]{:S(2)}) copy-start(bf16[512,2048]{1,0:T(8,128)(2,1)} %param.25) | copy-start | bytes 6291460
  (81 other events, 929.8 us)
Sparse Core Ops, SparseCore 0:
  53.2 157.6 all-reduce.16
  254.4 153.9 all-reduce.18
  519.6 290.5 all-reduce.22
  863.5 40.2 reduce-scatter.9
  947.3 40.2 reduce-scatter.5
  990.9 71.2 reduce-scatter.13
  1066.0 71.2 reduce-scatter.11
  1143.4 565.9 all-reduce.20
  1712.2 137.0 reduce-scatter.7
where the time goes:
time: 1870 us; the launch traced here: 1860 us
  waiting for transfers between devices  1150 us (61%)
  matrix products  441 us (24%)
  other arithmetic  170 us (9%)
  blocking collectives  68.7 us (4%)
    psum x1, waiting for transfers between devices, forward_block(): summed = lax.psum(down_part.astype(jnp.bfloat16), 'tp').astype(jnp.float32)  496 us
    psum x2, waiting for transfers between devices, forward_block(): lax.psum(partial_value.astype(jnp.bfloat16), 'tp').astype(jnp.float32)  311 us
    psum x1, waiting for transfers between devices, backward_block(): lax.psum(partial2.astype(jnp.bfloat16), 'tp').astype(jnp.float32)  290 us
    unnamed x2, blocking collectives  68.7 us
    dot_general x2, matrix products, backward_block(): jnp.einsum('hst,shd->td', grad_scores, heads_q, preferred_element_type=jn...  51.7 us
    dot_general x2, matrix products, backward_block(): jnp.einsum('hst,td->shd', grad_scores, keys_low, preferred_element_type=j...  50.1 us
    reduce_sum x4, other arithmetic, layer_norm(): return center * lax.rsqrt(spread + 1e-05) * gain_vec + shift_vec  49.5 us
    reduce_scatter x1, waiting for transfers between devices, reduce_once(): lax.psum_scatter(grad_terms[12], ('dp', 'tp'), scatter_dimension=0, tiled...  48.8 us
  transfers between devices with their start and end apart: 9, of which 5 were waited for; matrix products, arithmetic and copies ran while one was open for 20% of the time, Pallas kernels for 0%

commit v1 on v0

--- a/solution.py
+++ b/solution.py
@@ -65,7 +65,13 @@
     )
     activated = gelu_tanh(before).astype(jnp.bfloat16)
     down_part = jnp.dot(activated, params["down_weight"], preferred_element_type=jnp.float32)
-    summed = lax.psum(down_part.astype(jnp.bfloat16), "tp").astype(jnp.float32)
+
+    def read_points_up(load, which_axis):
+        base_arr = jax.lax.all_gather(load, which_axis)
+        tmp = jnp.sum(base_arr, axis=0)
+        return tmp
+
+    summed = read_points_up(down_part.astype(jnp.bfloat16), "tp").astype(jnp.float32)
     result = hidden1 + summed + params["down_bias"]
     kept_state = (
         normed1,

time: 1870 us -> 2010 us (1.075)
  waiting for transfers between devices: 1150 us -> 1260 us
  other arithmetic: 170 us -> 196 us
    all_gather x0 -> x2, waiting for transfers between devices: none -> 380 us  [read_points_up(): base_arr = jax.lax.all_gather(load, which_axis)]
    psum x1, waiting for transfers between devices: 496 us -> 228 us  [backward_block(): lax.psum(partial1.astype(jnp.bfloat16), 'tp').astype(jnp.float32)]
    reduce_sum x0 -> x2, other arithmetic: none -> 25.7 us  [read_points_up(): tmp = jnp.sum(base_arr, axis=0)]
  transfers between devices with their start and end apart: 9 -> 11, of which waited for: 5 -> 7; matrix products, arithmetic and copies ran while one was open for 20% -> 25% of each run, Pallas kernels for 0% -> 0%
where the time goes in v1:
time: 2010 us; the launch traced here: 2000 us
  waiting for transfers between devices  1260 us (63%)
  matrix products  441 us (22%)
  other arithmetic  196 us (10%)
  blocking collectives  69.3 us (3%)
    all_gather x2, waiting for transfers between devices, read_points_up(): base_arr = jax.lax.all_gather(load, which_axis)  380 us
    psum x2, waiting for transfers between devices, forward_block(): lax.psum(partial_value.astype(jnp.bfloat16), 'tp').astype(jnp.float32)  311 us
    psum x1, waiting for transfers between devices, backward_block(): lax.psum(partial2.astype(jnp.bfloat16), 'tp').astype(jnp.float32)  280 us
    psum x1, waiting for transfers between devices, backward_block(): lax.psum(partial1.astype(jnp.bfloat16), 'tp').astype(jnp.float32)  228 us
    unnamed x2, blocking collectives  69.3 us
    reduce_scatter x1, waiting for transfers between devices, reduce_once(): lax.psum_scatter(grad_terms[12], ('dp', 'tp'), scatter_dimension=0, tiled...  63.5 us
    dot_general x2, matrix products, backward_block(): jnp.einsum('hst,td->shd', grad_scores, keys_low, preferred_element_type=j...  55.1 us
    reduce_sum x4, other arithmetic, layer_norm(): return center * lax.rsqrt(spread + 1e-05) * gain_vec + shift_vec  51.7 us
  transfers between devices with their start and end apart: 11, of which 7 were waited for; matrix products, arithmetic and copies ran while one was open for 25% of the time, Pallas kernels for 0%

profile of v1, /device:TPU:0, one launch (start us, length us, event | category | flops | bytes accessed | tf_op | source)
XLA Modules:
  0.0 2003.5 jit_solution(3909376264718276176)
XLA Ops:
  53.8 157.1 %all-reduce.17.cloned.1.call-done = bf16[1024,2048]{1,0:T(8,128)(2,1)} async-done(((bf16[1024,2048]{1,0:T(8,128)(2,1)}), bf16[1024,2048]{1,0:T(8,128)(2,1)}) %all-reduce.17.cloned.1.call-update) | async-done | bytes 4194320 | tf_op jit(solution)/shard_map/psum | solution.py:59
  241.0 17.0 fusion.100
  263.7 154.0 %all-reduce.19.cloned.1.call-done = bf16[1024,2048]{1,0:T(8,128)(2,1)} async-done(((bf16[1024,2048]{1,0:T(8,128)(2,1)}), bf16[1024,2048]{1,0:T(8,128)(2,1)}) %all-reduce.19.cloned.1.call-update) | async-done | bytes 4194320 | tf_op jit(solution)/shard_map/psum | solution.py:59
  458.7 14.4 fusion.161
  476.8 14.5 convolution_convert_fusion.4
  491.4 19.6 convert_reduce_fusion.8
  526.4 20.9 %convert_reduce_fusion.9 = (f32[2048]{0:T(1024)}, bf16[1024,2048]{1,0:T(8,128)(2,1)}) fusion(f32[1024,2048]{1,0:T(8,128)} %copy-done.93, f32[2048]{0:T(1024)S(1)} %convert_element_type.321, bf16[2048,2048]{1,0:T(8,128)(2,1)} %param.31, bf16[2048,2048]{1,0:T(8,128)(2,1)} %param.33), kind=kOutput, calls=%fused_computation.107 | convolution fusion | flops 8638167040 | bytes 25182208 | tf_op jit(solution)/shard_map/dot_general | solution.py:110
  559.4 20.4 %fusion.85 = f32[2048,2048]{1,0:T(8,128)} fusion(bf16[2048,2048]{1,0:T(8,128)(2,1)} %param.33, f32[1024,2048]{1,0:T(8,128)} %copy-done.93, f32[2048]{0:T(1024)S(1)} %convert_element_type.321), kind=kOutput, calls=%fused_computation.150 | convolution fusion | flops 8610906112 | bytes 29368320 | tf_op jit(solution)/shard_map/dot_general | solution.py:109
  579.8 21.9 %add_convert_fusion = bf16[2048,2048]{1,0:T(8,128)(2,1)} fusion(f32[2048,2048]{1,0:T(8,128)} %fusion.85, bf16[2048,2048]{1,0:T(8,128)(2,1)} %param.33, f32[1024,2048]{1,0:T(8,128)} %copy-done.92, f32[2048]{0:T(1024)S(1)} %convert_element_type.321), kind=kOutput, calls=%fused_computation.14 | convolution fusion | flops 8619294720 | bytes 37756928 | tf_op jit(solution)/shard_map/dot_general | solution.py:109
  602.4 17.4 fusion.160
  619.8 17.6 add_convert_fusion.1
  638.3 106.2 %all-gather.7.cloned.1.call-done = bf16[4096,2048]{1,0:T(8,128)(2,1)} async-done(((bf16[1024,2048]{1,0:T(8,128)(2,1)}), bf16[4096,2048]{1,0:T(8,128)(2,1)}) %all-gather.7.cloned.1.call-update) | async-done | bytes 16777232 | tf_op jit(solution)/shard_map/all_gather | solution.py:70
  757.5 273.4 %all-gather.5.cloned.1.call-done = bf16[4096,2048]{1,0:T(8,128)(2,1)} async-done(((bf16[1024,2048]{1,0:T(8,128)(2,1)}), bf16[4096,2048]{1,0:T(8,128)(2,1)}) %all-gather.5.cloned.1.call-update) | async-done | bytes 16777232 | tf_op jit(solution)/shard_map/all_gather | solution.py:70
  1043.6 279.5 %all-reduce.23.cloned.1.call-done = (bf16[1024,2048]{1,0:T(8,128)(2,1)}, bf16[1024,2048]{1,0:T(8,128)(2,1)}) async-done(((bf16[1024,2048]{1,0:T(8,128)(2,1)}, bf16[1024,2048]{1,0:T(8,128)(2,1)}), (bf16[1024,2048]{1,0:T(8,128)(2,1)}, bf16[1024,2048]{1,0:T(8,128)(2,1)})) %all-reduce.23.cloned.1.call-update) | async-done | bytes 8388624 | tf_op jit(solution)/shard_map/psum | solution.py:115
  1323.2 17.7 fusion.33
  1403.5 29.3 %convert_reduce_fusion.10 = (f32[128,4]{0,1:T(4,128)S(1)}, bf16[128,4,1024]{2,0,1:T(8,128)(2,1)}) fusion(f32[1024,1024,4]{1,0,2:T(8,128)} %fusion.135, f32[4,1024,1024]{1,2,0:T(8,128)} %get-tuple-element.71, f32[4,1024]{1,0:T(4,128)S(1)} %log_add_fusion, f32[1024,256]{1,0:T(8,128)S(1)} %copy-done.30), kind=kOutput, calls=%fused_computation.155 | convolution fusion | flops 1104679424 | bytes 68454400 | tf_op jit(solution)/shard_map/hst,td->shd/dot_general | solution.py:137
  1432.8 25.8 %convert_reduce_fusion.11 = (f32[128,4]{0,1:T(4,128)S(1)}, bf16[128,4,1024]{2,0,1:T(8,128)(2,1)}) fusion(f32[1024,1024,4]{1,0,2:T(8,128)} %fusion.138, f32[4,1024,1024]{1,2,0:T(8,128)} %get-tuple-element.69, f32[4,1024]{1,0:T(4,128)S(1)} %log_add_fusion.1, f32[1024,256]{1,0:T(8,128)} %copy-done.27), kind=kOutput, calls=%fused_computation.156 | convolution fusion | flops 1104679424 | bytes 68454400 | tf_op jit(solution)/shard_map/hst,td->shd/dot_general | solution.py:137
  1458.6 23.1 %fusion.123 = bf16[1024,128]{0,1:T(8,128)(2,1)S(1)} fusion(bf16[1024,4,128]{0,2,1:T(8,128)(2,1)S(1)} %bitcast.210, f32[1024,1024,4]{1,0,2:T(8,128)} %fusion.135, f32[4,1024,1024]{1,2,0:T(8,128)} %get-tuple-element.71, f32[4,1024]{1,0:T(4,128)S(1)} %log_add_fusion), kind=kOutput, calls=%fused_computation.179 | convolution fusion | flops 1103238144 | bytes 34881536 | tf_op jit(solution)/shard_map/hst,shd->td/dot_general | solution.py:141
  1502.2 23.9 %fusion.122 = bf16[1024,128]{0,1:T(8,128)(2,1)} fusion(bf16[1024,4,128]{0,2,1:T(8,128)(2,1)S(1)} %bitcast.208, f32[1024,1024,4]{1,0,2:T(8,128)} %fusion.138, f32[4,1024,1024]{1,2,0:T(8,128)} %get-tuple-element.69, f32[4,1024]{1,0:T(4,128)S(1)} %log_add_fusion.1), kind=kOutput, calls=%fused_computation.178 | convolution fusion | flops 1103238144 | bytes 34881536 | tf_op jit(solution)/shard_map/hst,shd->td/dot_general | solution.py:141
  1563.9 43.4 %all-reduce.3 = f32[128]{0:T(128)S(1)} all-reduce(f32[128]{0:T(128)S(1)} %add.339), channel_id=9, replica_groups=mesh['dp'=8,'tp'=4] {'dp','tp'}, use_global_device_ids=true, to_apply=%region_43.44.clone | all-reduce | flops 128 | bytes 1024
  1628.8 227.8 %all-reduce.21.cloned.1.call-done = (bf16[1024,2048]{1,0:T(8,128)(2,1)}, bf16[1024,2048]{1,0:T(8,128)(2,1)}) async-done(((bf16[1024,2048]{1,0:T(8,128)(2,1)}, bf16[1024,2048]{1,0:T(8,128)(2,1)}), (bf16[1024,2048]{1,0:T(8,128)(2,1)}, bf16[1024,2048]{1,0:T(8,128)(2,1)})) %all-reduce.21.cloned.1.call-update) | async-done | bytes 8388624 | tf_op jit(solution)/shard_map/psum | solution.py:151
  1876.9 25.8 %all-reduce.9 = (bf16[2048]{0:T(1024)(128)(2,1)S(1)}, bf16[2048]{0:T(1024)(128)(2,1)S(1)}, bf16[512]{0:T(512)(128)(2,1)S(1)}, bf16[2048]{0:T(1024)(128)(2,1)S(1)...) all-reduce(bf16[2048]{0:T(1024)(128)(2,1)S(1)} %add_convert_fusion., ...), channel_id=4, replica_groups=mesh['dp'=8,'tp'=4] {'dp'}, use_global_device_ids=true, to_apply=%region_32.33.clone | all-reduce | flops 14848 | bytes 59392
  1907.7 16.7 add_convert_fusion.4
  1933.0 63.5 %reduce-scatter.8.cloned.1.call-done = f32[64,256]{1,0:T(8,128)} async-done(((f32[2048,256]{1,0:T(8,128)}), f32[64,256]{1,0:T(8,128)}) %reduce-scatter.8.cloned.1.call-update) | async-done | bytes 65552 | tf_op jit(solution)/shard_map/reduce_scatter | solution.py:216
  (348 shorter events, 355.2 us)
Async XLA Ops:
  7.2 203.8 %all-reduce.17.cloned.1.call-start = ((), (), s32[]{:S(2)}) async-start(), calls=%async_computation.5 | async-start | bytes 8388608 | tf_op jit(solution)/shard_map/psum | solution.py:59
  8.1 232.9 %copy-start.80 = (f32[128]{0:T(128)}, f32[128]{0:T(128)S(1)}, u32[]{:S(2)}) copy-start(f32[128]{0:T(128)S(1)} %convert_element_type.308) | copy-start | bytes 1540
  13.0 204.2 %copy-start.33 = (f32[2048]{0:T(1024)}, f32[2048]{0:T(1024)S(1)}, u32[]{:S(2)}) copy-start(f32[2048]{0:T(1024)S(1)} %convert_element_type.305) | copy-start | bytes 24580
  53.1 364.5 %all-reduce.19.cloned.1.call-start = ((), (), s32[]{:S(2)}) async-start(), calls=%async_computation.6 | async-start | bytes 8388608 | tf_op jit(solution)/shard_map/psum | solution.py:59
  53.2 405.4 %copy-start.31 = (f32[2048]{0:T(1024)}, f32[2048]{0:T(1024)S(1)}, u32[]{:S(2)}) copy-start(f32[2048]{0:T(1024)S(1)} %convert_element_type.317) | copy-start | bytes 24580
  53.2 168.5 %copy-start.38 = (f32[1024]{0:T(1024)}, f32[1024]{0:T(1024)S(1)}, u32[]{:S(2)}) copy-start(f32[1024]{0:T(1024)S(1)} %broadcast_multiply_fusion.1) | copy-start | bytes 12292
  263.5 481.0 %all-gather.7.cloned.1.call-start = ((), (), s32[]{:S(2)}) async-start(), calls=%async_computation.13 | async-start | bytes 20971520 | tf_op jit(solution)/shard_map/all_gather | solution.py:70
  263.6 195.1 %copy-start.44 = (f32[2048]{0:T(1024)}, f32[2048]{0:T(1024)S(1)}, u32[]{:S(2)}) copy-start(f32[2048]{0:T(1024)S(1)} %convert_element_type.318) | copy-start | bytes 24580
  263.6 195.0 %copy-start.70 = (f32[2048]{0:T(1024)}, f32[2048]{0:T(1024)S(1)}, u32[]{:S(2)}) copy-start(f32[2048]{0:T(1024)S(1)} %convert_element_type.319) | copy-start | bytes 24580
  263.6 195.0 %copy-start.48 = (f32[1024]{0:T(1024)}, f32[1024]{0:T(1024)S(1)}, u32[]{:S(2)}) copy-start(f32[1024]{0:T(1024)S(1)} %broadcast_multiply_fusion.2) | copy-start | bytes 12292
  458.6 572.4 %all-gather.5.cloned.1.call-start = ((), (), s32[]{:S(2)}) async-start(), calls=%async_computation.12 | async-start | bytes 20971520 | tf_op jit(solution)/shard_map/all_gather | solution.py:70
  491.3 831.8 %all-reduce.23.cloned.1.call-start = ((), (), s32[]{:S(2)}) async-start(), calls=%async_computation.15 | async-start | bytes 16777216 | tf_op jit(solution)/shard_map/psum | solution.py:115
  559.4 999.0 %reduce-scatter.14.cloned.1.call-start = ((), (), s32[]{:S(2)}) async-start(), calls=%async_computation.11 | async-start | bytes 9437184 | tf_op jit(solution)/shard_map/reduce_scatter | solution.py:211
  601.7 959.4 %reduce-scatter.12.cloned.1.call-start = ((), (), s32[]{:S(2)}) async-start(), calls=%async_computation.10 | async-start | bytes 9437184 | tf_op jit(solution)/shard_map/reduce_scatter | solution.py:179
  637.5 987.6 %reduce-scatter.10.cloned.1.call-start = ((), (), s32[]{:S(2)}) async-start(), calls=%async_computation.9 | async-start | bytes 2359296 | tf_op jit(solution)/shard_map/reduce_scatter | solution.py:208
  1403.5 223.5 %reduce-scatter.6.cloned.1.call-start = ((), (), s32[]{:S(2)}) async-start(), calls=%async_computation.7 | async-start | bytes 2359296 | tf_op jit(solution)/shard_map/reduce_scatter | solution.py:176
  1481.7 54.4 %copy-start.25 = (bf16[1024,128]{0,1:T(8,128)(2,1)}, bf16[1024,128]{0,1:T(8,128)(2,1)S(1)}, u32[]{:S(2)}) copy-start(bf16[1024,128]{0,1:T(8,128)(2,1)S(1)} %fusion.123) | copy-start | bytes 786436
  1502.1 354.5 %all-reduce.21.cloned.1.call-start = ((), (), s32[]{:S(2)}) async-start(), calls=%async_computation.14 | async-start | bytes 16777216 | tf_op jit(solution)/shard_map/psum | solution.py:151
  1551.9 56.1 %copy-start.35 = (bf16[1024,128]{0,1:T(8,128)(2,1)S(1)}, bf16[1024,128]{0,1:T(8,128)(2,1)}, u32[]{:S(2)}) copy-start(bf16[1024,128]{0,1:T(8,128)(2,1)} %fusion.122) | copy-start | bytes 786436
  1551.9 444.6 %reduce-scatter.8.cloned.1.call-start = ((), (), s32[]{:S(2)}) async-start(), calls=%async_computation.8 | async-start | bytes 2162688 | tf_op jit(solution)/shard_map/reduce_scatter | solution.py:216
  1558.3 53.2 %copy-start.26 = (bf16[1024,128]{0,1:T(8,128)(2,1)S(1)}, bf16[1024,128]{0,1:T(8,128)(2,1)}, u32[]{:S(2)}) copy-start(bf16[1024,128]{0,1:T(8,128)(2,1)} %copy-done.25) | copy-start | bytes 786436
  1616.6 240.0 %copy-start.34 = (f32[2048]{0:T(1024)S(1)}, f32[2048]{0:T(1024)}, u32[]{:S(2)}) copy-start(f32[2048]{0:T(1024)} %copy-done.33) | copy-start | bytes 24580
  1616.6 240.0 %copy-start.37 = (f32[1024]{0:T(1024)S(1)}, f32[1024]{0:T(1024)}, u32[]{:S(2)}) copy-start(f32[1024]{0:T(1024)} %copy-done.36) | copy-start | bytes 12292
  1616.6 240.0 %copy-start.39 = (f32[1024]{0:T(1024)S(1)}, f32[1024]{0:T(1024)}, u32[]{:S(2)}) copy-start(f32[1024]{0:T(1024)} %copy-done.38) | copy-start | bytes 12292
  (96 other events, 962.6 us)
Sparse Core Ops, SparseCore 0:
  53.2 157.6 all-reduce.16
  263.6 153.9 all-reduce.18
  458.7 285.7 all-gather.6
  745.9 284.9 all-gather.4
  1033.4 289.7 all-reduce.22
  1326.4 70.2 reduce-scatter.13
  1400.6 71.2 reduce-scatter.11
  1475.2 41.3 reduce-scatter.9
  1520.3 41.2 reduce-scatter.5
  1564.0 292.5 all-reduce.20
  1859.4 137.0 reduce-scatter.7
